TPU v7x, 32 devices: a whole 2x2x4 slice. The times are simulated.
32 devices in a mesh: section: 2 (over core), seq: 4 (over z), fsdp: 4 (over y, x).
Axes of the slice: x: 2, y: 2, z: 4, core: 2. Of those that a mesh axis runs over, the one named last changes fastest.
Arguments:
- inputs: float32 [2, 4, 512, 768], P(None, 'fsdp', 'seq'), may hold values from -6 to 6
- out_grad: float32 [2, 4, 512, 768], P(None, 'fsdp', 'seq'), may hold values from -6 to 6
- norm_gain: bfloat16 [2, 768], P('section', 'fsdp'), may hold values from 0.099609375 to 1.8984375
- input_weight: bfloat16 [2, 768, 3328], P('section', 'fsdp'), may hold values from -0.21875 to 0.21875
- conv_weight: bfloat16 [2, 4, 1792], P('section', None, 'fsdp'), may hold values from -3 to 3
- conv_bias: bfloat16 [2, 1792], P('section', 'fsdp'), may hold values from -3 to 3
- skip_gain: bfloat16 [2, 24], P('section', 'fsdp'), may hold values from 1 to 4
- gate_gain: bfloat16 [2, 1536], P('section', 'fsdp'), may hold values from 0.099609375 to 1.8984375
- out_weight: bfloat16 [2, 1536, 768], P('section', 'fsdp'), may hold values from -0.15625 to 0.15625
- step_codes: int32 [2, 2, 4, 512, 24], P('section', None, 'fsdp', 'seq'), may hold values from 128 to 512
- decay_codes: int32 [2, 2, 4, 512, 24], P('section', None, 'fsdp', 'seq'), may hold values from 2 to 45000, as said below
Outputs:
- section_outputs: float32 [2, 2, 4, 512, 768], P('section', None, 'fsdp', 'seq')
- section_input_grads: float32 [2, 2, 4, 512, 768], P('section', None, 'fsdp', 'seq')
- norm_gain_grad: float32 [2, 768], P('section', 'fsdp')
- in_weight_grad: float32 [2, 768, 3328], P('section', 'fsdp')
- conv_weight_grad: float32 [2, 4, 1792], P('section', None, 'fsdp')
- conv_bias_grad: float32 [2, 1792], P('section', 'fsdp')
- skip_gain_grad: float32 [2, 24], P('section', 'fsdp')
- gate_gain_grad: float32 [2, 1536], P('section', 'fsdp')
- out_weight_grad: float32 [2, 1536, 768], P('section', 'fsdp')
Inputs may be any that keep to these rules, and one draw needn't show every extreme that they name: `decay_codes`: codes are positive.
All inputs are finite; a program needn't handle non-finite values.
Results may differ from a plain program's by a relative error of at most 0.012.
Values may be sent and summed in bfloat16 or wider, within the bound.
A program may use at most 256 MiB of HBM per device.

v0:
```python
import jax
import jax.numpy as jnp
from jax import lax
from jax.sharding import PartitionSpec as P

DI = 1536
HEADS = 24
HEAD_DIM = 64
STATE = 128
CONV = 4


EPSILON = 1e-05
STEP_SCALE = 256.0
DECAY_SCALE = 65536.0
HIGHEST = lax.Precision.HIGHEST


def passed_along(x, axis, by):
    size = lax.axis_size(axis)
    pairs = [(i, i + by) for i in range(size) if 0 <= i + by < size]
    return lax.ppermute(x, axis, pairs)


def prefix(value, axis, join, neutral, backward):
    count, mine = (lax.axis_size(axis), lax.axis_index(axis))
    pieces = jax.tree.map(lambda part: lax.all_gather(part, axis), value)
    if backward:
        pieces = jax.tree.map(lambda part: part[::-1], pieces)
        mine = count - 1 - mine
    total = jax.tree.map(
        lambda part, zero: jnp.full_like(part, 0) + jnp.asarray(zero, part.dtype), value, neutral
    )

    def hop(position, total):
        longer = join(total, jax.tree.map(lambda part: part[position], pieces))
        return jax.tree.map(lambda new, old: jnp.where(position < mine, new, old), longer, total)

    return lax.fori_loop(0, count - 1, hop, total)


def norm_input(hidden, gain_vector):
    inverse_rms = lax.rsqrt(jnp.mean(hidden * hidden, axis=-1, keepdims=True) + EPSILON)
    return hidden * inverse_rms * gain_vector


def gated_norm(mixer_out, gate_outputs, gain_vector):
    gated_products = mixer_out * jax.nn.silu(gate_outputs)
    inverse_rms = lax.rsqrt(
        jnp.mean(gated_products * gated_products, axis=-1, keepdims=True) + EPSILON
    )
    return gated_products * inverse_rms * gain_vector


def conv_silu(before, current, kernel, offset):
    extended = jnp.concatenate([before, current], axis=0)
    length = current.shape[0]
    summed = offset[None, :] + kernel[0][None, :] * extended[0:length]
    for shift_row in range(1, kernel.shape[0]):
        summed = summed + kernel[shift_row][None, :] * extended[shift_row : shift_row + length]
    return jax.nn.silu(summed)


def split_mixer(conv_part):
    length = conv_part.shape[0]
    head_values = conv_part[:, :DI].reshape(length, HEADS, HEAD_DIM)
    input_keys = conv_part[:, DI : DI + STATE]
    output_queries = conv_part[:, DI + STATE :]
    return (head_values, input_keys, output_queries)


def step_and_decay(step_block, decay_block):
    step_sizes = step_block.astype(jnp.float32) / STEP_SCALE
    cumulative = jnp.cumsum(-decay_block.astype(jnp.float32) / DECAY_SCALE, axis=0)
    return (step_sizes, cumulative)


def block_summary(head_values, input_keys, step_sizes, cumulative):
    to_end = jnp.exp(cumulative[-1][None, :] - cumulative) * step_sizes
    return jnp.einsum("sh,shp,sn->hpn", to_end, head_values, input_keys, precision=HIGHEST)


def block_output(
    head_values, input_keys, output_queries, step_sizes, cumulative, entering, skip_weights
):
    length = head_values.shape[0]
    later = lax.broadcasted_iota(jnp.int32, (length, length), 0)
    earlier = lax.broadcasted_iota(jnp.int32, (length, length), 1)
    causal = (later >= earlier)[None, :, :]
    cum_heads = cumulative.T
    dispersion_width = cum_heads[:, :, None] - cum_heads[:, None, :]
    decays = jnp.where(causal, jnp.exp(jnp.where(causal, dispersion_width, 0.0)), 0.0)
    scores = jnp.dot(output_queries, input_keys.T, precision=HIGHEST)
    coupling = decays * scores[None, :, :] * step_sizes.T[:, None, :]
    within = jnp.einsum("hts,shp->thp", coupling, head_values, precision=HIGHEST)
    carried = jnp.exp(cumulative)[:, :, None] * jnp.einsum(
        "tn,hpn->thp", output_queries, entering, precision=HIGHEST
    )
    return within + carried + skip_weights[None, :, None] * head_values


def combine_states(earlier, later):
    return (earlier[0] + later[0], jnp.exp(later[0])[:, None, None] * earlier[1] + later[1])


def front_part(hidden, params):
    normed = norm_input(hidden, params[1].astype(jnp.float32)).astype(jnp.bfloat16)
    projected = jnp.dot(normed, params[0], preferred_element_type=jnp.float32)
    return (normed, projected[:, :DI], projected[:, DI:])


def layer_forward(hidden, params, step_block, decay_block):
    normed, gate_outputs, mixer_rows = front_part(hidden, params)
    before = passed_along(mixer_rows[-(CONV - 1) :], "seq", 1)
    conv_part = conv_silu(
        before, mixer_rows, params[2].astype(jnp.float32), params[3].astype(jnp.float32)
    )
    head_values, input_keys, output_queries = split_mixer(conv_part)
    step_sizes, cumulative = step_and_decay(step_block, decay_block)
    summary = block_summary(head_values, input_keys, step_sizes, cumulative)
    start = (jnp.zeros((HEADS,), jnp.float32), jnp.zeros_like(summary))
    entering = prefix((cumulative[-1], summary), "seq", combine_states, start, False)[1]
    mixed = block_output(
        head_values,
        input_keys,
        output_queries,
        step_sizes,
        cumulative,
        entering,
        params[4].astype(jnp.float32),
    )
    mixer_out = mixed.reshape(hidden.shape[0], DI)
    normed_out = gated_norm(mixer_out, gate_outputs, params[5].astype(jnp.float32)).astype(
        jnp.bfloat16
    )
    result = hidden + jnp.dot(normed_out, params[6], preferred_element_type=jnp.float32)
    return (result, before, entering)


def layer_backward(hidden, before, entering, step_block, decay_block, out_cot, params):
    length = hidden.shape[0]
    normed, gate_outputs, mixer_rows = front_part(hidden, params)
    kernel = params[2].astype(jnp.float32)
    offset = params[3].astype(jnp.float32)
    conv_part, conv_vjp = jax.vjp(conv_silu, before, mixer_rows, kernel, offset)
    head_values, input_keys, output_queries = split_mixer(conv_part)
    step_sizes, cumulative = step_and_decay(step_block, decay_block)

    def mixer_fn(values_in, keys_in, queries_in, skip_in):
        mixed_here = block_output(
            values_in, keys_in, queries_in, step_sizes, cumulative, entering, skip_in
        )
        return (mixed_here, block_summary(values_in, keys_in, step_sizes, cumulative))

    (mixed, _), mixer_vjp = jax.vjp(
        mixer_fn, head_values, input_keys, output_queries, params[4].astype(jnp.float32)
    )
    mixer_out = mixed.reshape(length, DI)
    normed_out, norm_vjp = jax.vjp(
        gated_norm, mixer_out, gate_outputs, params[5].astype(jnp.float32)
    )
    out_rounded = normed_out.astype(jnp.bfloat16)
    cot_rounded = out_cot.astype(jnp.bfloat16)
    grad_normed_out = jnp.dot(cot_rounded, params[6].T, preferred_element_type=jnp.float32)
    grad_mixer, grad_gate, grad_gate_gain = norm_vjp(grad_normed_out)
    grad_heads = grad_mixer.reshape(length, HEADS, HEAD_DIM)
    local_entry = jnp.einsum(
        "th,thp,tn->hpn", jnp.exp(cumulative), grad_heads, output_queries, precision=HIGHEST
    )
    start = (jnp.zeros((HEADS,), jnp.float32), jnp.zeros_like(local_entry))
    leaving = prefix((cumulative[-1], local_entry), "seq", combine_states, start, True)[1]
    grad_values, grad_keys, grad_queries, grad_skip = mixer_vjp((grad_heads, leaving))
    grad_conv = jnp.concatenate([grad_values.reshape(length, DI), grad_keys, grad_queries], axis=1)
    grad_before, grad_rows, grad_kernel, grad_offset = conv_vjp(grad_conv)
    upstream_adjoint = passed_along(grad_before, "seq", -1)
    grad_rows = grad_rows.at[-(CONV - 1) :].add(upstream_adjoint)
    grad_projected = jnp.concatenate([grad_gate, grad_rows], axis=1).astype(jnp.bfloat16)
    grad_normed = jnp.dot(grad_projected, params[0].T, preferred_element_type=jnp.float32)
    _, input_vjp = jax.vjp(norm_input, hidden, params[1].astype(jnp.float32))
    grad_hidden, grad_norm_gain = input_vjp(grad_normed)
    smalls = (grad_norm_gain, grad_kernel, grad_offset, grad_skip, grad_gate_gain)
    factors = (normed, grad_projected, out_rounded, cot_rounded)
    return (out_cot + grad_hidden, smalls, factors)


def body(
    inputs,
    out_grad,
    norm_gain,
    input_weight,
    conv_weight,
    conv_bias,
    skip_gain,
    gate_gain,
    out_weight,
    step_codes,
    decay_codes,
):
    first_section = lax.axis_index("section") == 0
    micro_count = inputs.shape[0]
    shards = (
        input_weight[0],
        norm_gain[0],
        conv_weight[0],
        conv_bias[0],
        skip_gain[0],
        gate_gain[0],
        out_weight[0],
    )
    params = (
        lax.all_gather(shards[0], "fsdp", axis=0, tiled=True),
        lax.all_gather(shards[1], "fsdp", axis=0, tiled=True),
        lax.all_gather(shards[2], "fsdp", axis=1, tiled=True),
        lax.all_gather(shards[3], "fsdp", axis=0, tiled=True),
        lax.all_gather(shards[4], "fsdp", axis=0, tiled=True),
        lax.all_gather(shards[5], "fsdp", axis=0, tiled=True),
        lax.all_gather(shards[6], "fsdp", axis=0, tiled=True),
    )
    forward_results = []
    kept_ticks = []
    received = jnp.zeros_like(inputs[0, 0])
    for tick_index in range(micro_count + 1):
        early_mb = min(tick_index, micro_count - 1)
        late_mb = max(tick_index - 1, 0)
        hidden = jnp.where(first_section, inputs[early_mb, 0], received)
        step_block = jnp.where(first_section, step_codes[0, early_mb, 0], step_codes[0, late_mb, 0])
        decay_block = jnp.where(
            first_section, decay_codes[0, early_mb, 0], decay_codes[0, late_mb, 0]
        )
        result, before, entering = layer_forward(hidden, params, step_block, decay_block)
        forward_results.append(result)
        kept_ticks.append((hidden, before, entering, step_block, decay_block))
        if tick_index < micro_count:
            received = passed_along(result, "section", 1)
    small_sums = tuple((jnp.zeros(weight.shape, jnp.float32) for weight in params[1:6]))
    backward_results = []
    factor_ticks = []
    incoming = jnp.zeros_like(inputs[0, 0])
    for tick_index in range(micro_count + 1):
        late_kept = kept_ticks[min(tick_index, micro_count - 1) + 1]
        early_kept = kept_ticks[max(tick_index - 1, 0)]
        chosen = tuple(
            (
                jnp.where(first_section, early_piece, late_piece)
                for early_piece, late_piece in zip(early_kept, late_kept)
            )
        )
        adjoint_vector = jnp.where(
            first_section, incoming, out_grad[min(tick_index, micro_count - 1), 0]
        )
        active = jnp.where(first_section, tick_index >= 1, tick_index < micro_count)
        adjoint_vector = jnp.where(active, adjoint_vector, 0.0)
        grad_hidden, smalls, factors = layer_backward(
            chosen[0], chosen[1], chosen[2], chosen[3], chosen[4], adjoint_vector, params
        )
        small_sums = tuple((running + added for running, added in zip(small_sums, smalls)))
        factor_ticks.append(factors)
        backward_results.append(grad_hidden)
        if tick_index < micro_count:
            incoming = passed_along(grad_hidden, "section", -1)
    picked = [
        tuple(
            (
                jnp.where(first_section, later_piece, earlier_piece)
                for later_piece, earlier_piece in zip(
                    factor_ticks[index_mb + 1], factor_ticks[index_mb]
                )
            )
        )
        for index_mb in range(micro_count)
    ]
    normed_rows = jnp.concatenate([entry[0] for entry in picked], axis=0)
    projected_rows = jnp.concatenate([entry[1] for entry in picked], axis=0)
    output_rows = jnp.concatenate([entry[2] for entry in picked], axis=0)
    cotangent_rows = jnp.concatenate([entry[3] for entry in picked], axis=0)
    grad_in_weight = jnp.dot(normed_rows.T, projected_rows, preferred_element_type=jnp.float32)
    grad_out_weight = jnp.dot(output_rows.T, cotangent_rows, preferred_element_type=jnp.float32)
    totals = (
        grad_in_weight,
        small_sums[0],
        small_sums[1],
        small_sums[2],
        small_sums[3],
        small_sums[4],
        grad_out_weight,
    )
    shares = (
        lax.psum_scatter(totals[0], "fsdp", scatter_dimension=0, tiled=True),
        lax.psum_scatter(totals[1], "fsdp", scatter_dimension=0, tiled=True),
        lax.psum_scatter(totals[2], "fsdp", scatter_dimension=1, tiled=True),
        lax.psum_scatter(totals[3], "fsdp", scatter_dimension=0, tiled=True),
        lax.psum_scatter(totals[4], "fsdp", scatter_dimension=0, tiled=True),
        lax.psum_scatter(totals[5], "fsdp", scatter_dimension=0, tiled=True),
        lax.psum_scatter(totals[6], "fsdp", scatter_dimension=0, tiled=True),
    )
    reduced = lax.psum(
        (shares[0], shares[1], shares[2], shares[3], shares[4], shares[5], shares[6]), "seq"
    )
    outputs_section = jnp.stack(
        [
            jnp.where(first_section, forward_results[index_mb], forward_results[index_mb + 1])
            for index_mb in range(micro_count)
        ]
    )
    grads_section = jnp.stack(
        [
            jnp.where(first_section, backward_results[index_mb + 1], backward_results[index_mb])
            for index_mb in range(micro_count)
        ]
    )
    return (
        outputs_section[None, :, None],
        grads_section[None, :, None],
        reduced[1][None],
        reduced[0][None],
        reduced[2][None],
        reduced[3][None],
        reduced[4][None],
        reduced[5][None],
        reduced[6][None],
    )


def solution(mesh):
    return jax.shard_map(
        body,
        mesh=mesh,
        in_specs=(
            P(None, "fsdp", "seq", None),
            P(None, "fsdp", "seq", None),
            P("section", "fsdp"),
            P("section", "fsdp", None),
            P("section", None, "fsdp"),
            P("section", "fsdp"),
            P("section", "fsdp"),
            P("section", "fsdp"),
            P("section", "fsdp", None),
            P("section", None, "fsdp", "seq", None),
            P("section", None, "fsdp", "seq", None),
        ),
        out_specs=(
            P("section", None, "fsdp", "seq", None),
            P("section", None, "fsdp", "seq", None),
            P("section", "fsdp"),
            P("section", "fsdp", None),
            P("section", None, "fsdp"),
            P("section", "fsdp"),
            P("section", "fsdp"),
            P("section", "fsdp"),
            P("section", "fsdp", None),
        ),
        check_vma=False,
    )
```

profile of v0, /device:TPU:0, one launch (start us, length us, event | category | flops | bytes accessed | tf_op | source)
XLA Modules:
  0.0 1038.3 jit_solution(1958306126555306620)
XLA Ops:
  14.0 12.1 %all-reduce.34 = (bf16[768]{0:T(1024)(128)(2,1)S(1)}, bf16[1792]{0:T(1024)(128)(2,1)S(1)}, bf16[24]{0:T(256)(128)(2,1)}) all-reduce(bf16[768]{0:T(1024)(128)(2,1)S(1)} %dynamic-update-slice.10, bf16[1792]{0:T(1024)(128)(2,1)S(1)} %dynamic-update-slice.9, ...), channel_id=4, replica_groups=mesh['section'=2,'seq'=4,'fsdp'=4] {'fsdp'}, use_global_device_ids=true, to_apply=%add.25 | all-reduce | flops 2584 | bytes 10336
  27.0 18.0 %all-gather.1 = bf16[1,4,1792]{1,0,2:T(2,128)(2,1)S(1)} all-gather(bf16[1,4,448]{1,0,2:T(2,128)(2,1)S(1)} %copy.316), channel_id=3, replica_groups=mesh['section'=2,'seq'=4,'fsdp'=4] {'fsdp'}, dimensions={2}, use_global_device_ids=true | all-gather | bytes 17920 | tf_op jit(solution)/shard_map/all_gather | solution.py:213
  50.4 37.6 %slice_reduce_fusion.3 = (f32[1792]{0:T(1024)S(1)}, f32[1792]{0:T(1024)S(1)}, f32[1792]{0:T(1024)S(1)}, f32[1792]{0:T(1024)S(1)}) fusion(f32[1,4,1792]{1,0,2:T(1,128)S(1)} %convert_element_type.160), kind=kLoop, calls=%fused_computation.225 | loop fusion | bytes 57344 | tf_op jit(solution)/shard_map/slice | solution.py:58
  103.7 11.7 %all-gather.13 = f32[4,1,24]{2,1,0:T(1,128)S(1)} all-gather(f32[1,1,24]{2,1,0:T(1,128)S(1)} %get-tuple-element.965), channel_id=1, replica_groups=mesh['section'=2,'seq'=4,'fsdp'=4] {'seq'}, dimensions={0}, use_global_device_ids=true | all-gather | bytes 480 | tf_op jit(solution)/shard_map/all_gather | solution.py:27
  115.4 7.9 all-gather.6
  128.7 38.3 %all-gather.30.cloned.1.call-done = f32[96,64,128]{2,1,0:T(8,128)} async-done(((f32[24,64,128]{2,1,0:T(8,128)}), f32[96,64,128]{2,1,0:T(8,128)}) %all-gather.30.cloned.1.call-update) | async-done | bytes 3145744 | tf_op jit(solution)/shard_map/all_gather | solution.py:27
  174.8 30.1 %all-gather.32.cloned.1.call-done = bf16[1,1536,768]{2,1,0:T(8,128)(2,1)} async-done(((bf16[1,384,768]{2,1,0:T(8,128)(2,1)}), bf16[1,1536,768]{2,1,0:T(8,128)(2,1)}) %all-gather.32.cloned.1.call-update) | async-done | bytes 2359312 | tf_op jit(solution)/shard_map/all_gather | solution.py:217
  227.4 12.0 %all-gather.14 = f32[4,1,24]{2,1,0:T(1,128)S(1)} all-gather(f32[1,1,24]{2,1,0:T(1,128)S(1)} %copy-done.227), channel_id=1, replica_groups=mesh['section'=2,'seq'=4,'fsdp'=4] {'seq'}, dimensions={0}, use_global_device_ids=true | all-gather | bytes 480 | tf_op jit(solution)/shard_map/all_gather | solution.py:27
  245.2 44.3 %all-gather.34.cloned.1.call-done = f32[96,64,128]{2,1,0:T(8,128)} async-done(((f32[24,64,128]{2,1,0:T(8,128)}), f32[96,64,128]{2,1,0:T(8,128)}) %all-gather.34.cloned.1.call-update) | async-done | bytes 3145744 | tf_op jit(solution)/shard_map/all_gather | solution.py:27
  340.9 10.6 %all-gather.16 = f32[4,1,24]{2,1,0:T(1,128)} all-gather(f32[1,1,24]{2,1,0:T(1,128)} %get-tuple-element.959), channel_id=1, replica_groups=mesh['section'=2,'seq'=4,'fsdp'=4] {'seq'}, dimensions={0}, use_global_device_ids=true | all-gather | bytes 480 | tf_op jit(solution)/shard_map/all_gather | solution.py:27
  369.3 35.5 %all-gather.38.cloned.1.call-done = f32[96,64,128]{2,1,0:T(8,128)} async-done(((f32[24,64,128]{2,1,0:T(8,128)}), f32[96,64,128]{2,1,0:T(8,128)}) %all-gather.38.cloned.1.call-update) | async-done | bytes 3145744 | tf_op jit(solution)/shard_map/all_gather | solution.py:27
  408.8 6.5 while.90
  435.9 8.3 all-gather.15
  471.1 26.8 %all-gather.36.cloned.1.call-done = f32[96,64,128]{2,1,0:T(8,128)} async-done(((f32[24,64,128]{2,1,0:T(8,128)}), f32[96,64,128]{2,1,0:T(8,128)}) %all-gather.36.cloned.1.call-update) | async-done | bytes 3145744 | tf_op jit(solution)/shard_map/all_gather | solution.py:27
  518.8 8.9 all-gather.17
  556.6 24.4 %all-gather.40.cloned.1.call-done = f32[96,64,128]{2,1,0:T(8,128)} async-done(((f32[24,64,128]{2,1,0:T(8,128)}), f32[96,64,128]{2,1,0:T(8,128)}) %all-gather.40.cloned.1.call-update) | async-done | bytes 3145744 | tf_op jit(solution)/shard_map/all_gather | solution.py:27
  632.7 9.6 all-gather.18
  655.5 34.5 %all-gather.42.cloned.1.call-done = f32[96,64,128]{2,1,0:T(8,128)} async-done(((f32[24,64,128]{2,1,0:T(8,128)}), f32[96,64,128]{2,1,0:T(8,128)}) %all-gather.42.cloned.1.call-update) | async-done | bytes 3145744 | tf_op jit(solution)/shard_map/all_gather | solution.py:27
  693.9 7.8 while.92
  733.3 15.3 %reduce-scatter.8.cloned.1.call-done = f32[384,768]{1,0:T(8,128)} async-done(((f32[1536,768]{1,0:T(8,128)}), f32[384,768]{1,0:T(8,128)}) %reduce-scatter.8.cloned.1.call-update) | async-done | bytes 1179664 | tf_op jit(solution)/shard_map/reduce_scatter | solution.py:294
  748.6 104.4 %reduce-scatter.6.cloned.1.call-done = f32[192,3328]{1,0:T(8,128)} async-done(((f32[768,3328]{1,0:T(8,128)}), f32[192,3328]{1,0:T(8,128)}) %reduce-scatter.6.cloned.1.call-update) | async-done | bytes 2555920 | tf_op jit(solution)/shard_map/reduce_scatter | solution.py:288
  872.8 15.8 %all-reduce.31 = (f32[768]{0:T(1024)S(1)}, f32[1792]{0:T(1024)S(1)}, f32[24]{0:T(128)S(1)}, f32[1536]{0:T(1024)S(1)}) all-reduce(f32[768]{0:T(1024)S(1)} %add_add_fusion.12, f32[1792]{0:T(1024)S(1)} %add_add_fusion.11, f32[24]{0:T(128)S(1)} %add_add_fusion.13, ...), channel_id=15, replica_groups=mesh['section'=2,'seq'=4,'fsdp'=4] {'fsdp'}, use_global_device_ids=true, to_apply=%region_42.43.clone | all-reduce | flops 4120 | bytes 32960
  891.1 20.6 %all-reduce.32 = (f32[1,192]{1,0:T(1,128)}, f32[1,4,448]{2,1,0:T(4,128)}, f32[1,448]{1,0:T(1,128)}, f32[1,6]{1,0:T(1,128)}, f32[1,384]{1,0:T(1,128)}) all-reduce(f32[1,192]{1,0:T(1,128)S(1)} %bitcast.561, f32[1,4,448]{2,1,0:T(4,128)S(1)} %bitcast.556, ...), channel_id=1, replica_groups=mesh['section'=2,'seq'=4,'fsdp'=4] {'seq'}, use_global_device_ids=true, to_apply=%region_43.44 | all-reduce | flops 2822 | bytes 22576 | tf_op jit(solution)/shard_map/psum | solution.py:296
  911.8 115.0 %all-reduce.37.cloned.1.call-done = (f32[1,192,3328]{2,1,0:T(8,128)}, f32[1,384,768]{2,1,0:T(8,128)}) async-done(((f32[1,192,3328]{2,1,0:T(8,128)}, f32[1,384,768]{2,1,0:T(8,128)}), (f32[1,192,3328]{2,1,0:T(8,128)}, f32[1,384,768]{2,1,0:T(8,128)})) %all-reduce.37.cloned.1.call-update) | async-done | bytes 3735568 | tf_op jit(solution)/shard_map/psum | solution.py:296
  (822 shorter events, 391.2 us)
Async XLA Ops:
  7.2 80.9 %all-gather.28.cloned.1.call-start = ((), (), s32[]{:S(2)}) async-start(), calls=%async_computation.5 | async-start | bytes 6389760 | tf_op jit(solution)/shard_map/all_gather | solution.py:211
  7.9 159.1 %all-gather.30.cloned.1.call-start = ((), (), s32[]{:S(2)}) async-start(), calls=%async_computation.6 | async-start | bytes 3932160 | tf_op jit(solution)/shard_map/all_gather | solution.py:27
  92.6 4.9 collective-permute-start
  97.1 123.3 %copy-start.146 = (f32[1792]{0:T(1024)}, f32[1792]{0:T(1024)S(1)}, u32[]{:S(2)}) copy-start(f32[1792]{0:T(1024)S(1)} %convert_element_type.164) | copy-start | bytes 21508
  102.7 102.2 %all-gather.32.cloned.1.call-start = ((), (), s32[]{:S(2)}) async-start(), calls=%async_computation.7 | async-start | bytes 2949120 | tf_op jit(solution)/shard_map/all_gather | solution.py:217
  103.4 186.1 %all-gather.34.cloned.1.call-start = ((), (), s32[]{:S(2)}) async-start(), calls=%async_computation.8 | async-start | bytes 3932160 | tf_op jit(solution)/shard_map/all_gather | solution.py:27
  207.5 2.9 collective-permute-start.1
  215.4 5.1 collective-permute-start.2
  225.1 179.8 %all-gather.38.cloned.1.call-start = ((), (), s32[]{:S(2)}) async-start(), calls=%async_computation.10 | async-start | bytes 3932160 | tf_op jit(solution)/shard_map/all_gather | solution.py:27
  299.9 5.3 collective-permute-start.3
  309.8 3.4 collective-permute-start.4
  340.8 157.0 %all-gather.36.cloned.1.call-start = ((), (), s32[]{:S(2)}) async-start(), calls=%async_computation.9 | async-start | bytes 3932160 | tf_op jit(solution)/shard_map/all_gather | solution.py:27
  435.1 146.0 %all-gather.40.cloned.1.call-start = ((), (), s32[]{:S(2)}) async-start(), calls=%async_computation.11 | async-start | bytes 3932160 | tf_op jit(solution)/shard_map/all_gather | solution.py:27
  435.9 66.1 %copy-start.153 = (f32[128,24]{0,1:T(8,128)}, f32[128,24]{0,1:T(8,128)S(1)}, u32[]{:S(2)}) copy-start(f32[128,24]{0,1:T(8,128)S(1)} %copy.360) | copy-start | bytes 36868
  449.7 7.0 collective-permute-start.5
  463.6 5.9 collective-permute-start.6
  518.8 171.2 %all-gather.42.cloned.1.call-start = ((), (), s32[]{:S(2)}) async-start(), calls=%async_computation.12 | async-start | bytes 3932160 | tf_op jit(solution)/shard_map/all_gather | solution.py:27
  603.0 5.8 collective-permute-start.7
  615.2 3.9 collective-permute-start.8
  627.8 120.9 %reduce-scatter.8.cloned.1.call-start = ((), (), s32[]{:S(2)}) async-start(), calls=%async_computation.4 | async-start | bytes 5898240 | tf_op jit(solution)/shard_map/reduce_scatter | solution.py:294
  632.6 220.4 %reduce-scatter.6.cloned.1.call-start = ((), (), s32[]{:S(2)}) async-start(), calls=%async_computation.3 | async-start | bytes 12779520 | tf_op jit(solution)/shard_map/reduce_scatter | solution.py:288
  713.2 5.8 collective-permute-start.9
  726.5 163.5 %reduce-scatter.10.cloned.1.call-start = ((), (), s32[]{:S(2)}) async-start(), calls=%async_computation.13 | async-start | bytes 1146880
  731.7 295.1 %all-reduce.37.cloned.1.call-start = ((), (), s32[]{:S(2)}) async-start(), calls=%async_computation.14 | async-start | bytes 7471104 | tf_op jit(solution)/shard_map/psum | solution.py:296
  (233 other events, 1242.8 us)
Sparse Core Ops, SparseCore 0:
  9.8 69.3 all-gather.27
  102.8 64.1 all-gather.29
  168.9 35.9 all-gather.31
  225.2 64.2 all-gather.33
  341.0 63.8 all-gather.37
  435.2 62.5 all-gather.35
  518.9 62.1 all-gather.39
  627.9 62.0 all-gather.41
  692.9 55.6 reduce-scatter.7
  751.6 101.3 reduce-scatter.5
  856.5 27.2 reduce-scatter.9
  886.1 140.5 all-reduce.36
where the time goes:
time: 1050 us; the launch traced here: 1040 us
  waiting for transfers between devices  487 us (46%)
  matrix products  158 us (15%)
  blocking collectives  136 us (13%)
  local copies, waits for them, and re-layouts  134 us (13%)
  other arithmetic  80.2 us (8%)
  between operations  22.5 us (2%)
  starting transfers between devices  19.1 us (2%)
    all_gather x6, waiting for transfers between devices, prefix(): pieces = jax.tree.map(lambda part: lax.all_gather(part, axis), value)  204 us
    psum x1, waiting for transfers between devices, body(): lax.psum((shares[0], shares[1], shares[2], shares[3], shares[4], shares[5...  115 us
    reduce_scatter x1, waiting for transfers between devices, body(): lax.psum_scatter(totals[0], 'fsdp', scatter_dimension=0, tiled=True)  104 us
    all_gather x6, blocking collectives, prefix(): pieces = jax.tree.map(lambda part: lax.all_gather(part, axis), value)  61.1 us
    dot_general x12, matrix products, block_output(): jnp.einsum('hts,shp->thp', coupling, head_values, precision=HIGHEST)  41.1 us
    slice x1, local copies, waits for them, and re-layouts, conv_silu(): summed = offset[None, :] + kernel[0][None, :] * extended[0:length]  37.6 us
    all_gather x1, waiting for transfers between devices, body(): lax.all_gather(shards[6], 'fsdp', axis=0, tiled=True)  30.1 us
    unnamed x2, blocking collectives  27.9 us
  transfers between devices with their start and end apart: 22, of which 17 were waited for; matrix products, arithmetic and copies ran while one was open for 21% of the time, Pallas kernels for 0%

commit v1 on v0

v1 whole, which is shorter than its diff:
```python
import jax
import jax.numpy as jnp
from jax import lax
from jax.sharding import PartitionSpec as P

DI = 1536
HEADS = 24
HEAD_DIM = 64
STATE = 128
CONV = 4


EPSILON = 1e-05
STEP_SCALE = 256.0
DECAY_SCALE = 65536.0
HIGHEST = lax.Precision.HIGHEST


def passed_along(x, axis, by):
    size = lax.axis_size(axis)
    pairs = [(i, i + by) for i in range(size) if 0 <= i + by < size]
    return lax.ppermute(x, axis, pairs)


def carried_in(local, totals, backward):
    count, mine = (lax.axis_size("seq"), lax.axis_index("seq"))
    pieces = lax.all_gather(local.astype(jnp.bfloat16), "seq")
    source = lax.broadcasted_iota(jnp.int32, (count, count), 0)
    between = lax.broadcasted_iota(jnp.int32, (count, count), 1)
    if backward:
        inside = (between > mine) & (between < source)
        used = jnp.arange(count) > mine
    else:
        inside = (between > source) & (between < mine)
        used = jnp.arange(count) < mine
    decay = jnp.sum(jnp.where(inside[:, :, None], totals[None], 0.0), axis=1)
    weight = jnp.where(used[:, None], jnp.exp(decay), 0.0)
    return jnp.sum(weight[:, :, None, None] * pieces.astype(jnp.float32), axis=0)


def norm_input(hidden, gain_vector):
    inverse_rms = lax.rsqrt(jnp.mean(hidden * hidden, axis=-1, keepdims=True) + EPSILON)
    return hidden * inverse_rms * gain_vector


def gated_norm(mixer_out, gate_outputs, gain_vector):
    gated_products = mixer_out * jax.nn.silu(gate_outputs)
    inverse_rms = lax.rsqrt(
        jnp.mean(gated_products * gated_products, axis=-1, keepdims=True) + EPSILON
    )
    return gated_products * inverse_rms * gain_vector


def conv_silu(before, current, kernel, offset):
    extended = jnp.concatenate([before, current], axis=0)
    length = current.shape[0]
    summed = offset[None, :] + kernel[0][None, :] * extended[0:length]
    for shift_row in range(1, kernel.shape[0]):
        summed = summed + kernel[shift_row][None, :] * extended[shift_row : shift_row + length]
    return jax.nn.silu(summed)


def split_mixer(conv_part):
    length = conv_part.shape[0]
    head_values = conv_part[:, :DI].reshape(length, HEADS, HEAD_DIM)
    input_keys = conv_part[:, DI : DI + STATE]
    output_queries = conv_part[:, DI + STATE :]
    return (head_values, input_keys, output_queries)


def block_summary(head_values, input_keys, step_sizes, cumulative):
    to_end = jnp.exp(cumulative[-1][None, :] - cumulative) * step_sizes
    return jnp.einsum("sh,shp,sn->hpn", to_end, head_values, input_keys, precision=HIGHEST)


def block_output(
    head_values, input_keys, output_queries, step_sizes, cumulative, entering, skip_weights
):
    length = head_values.shape[0]
    later = lax.broadcasted_iota(jnp.int32, (length, length), 0)
    earlier = lax.broadcasted_iota(jnp.int32, (length, length), 1)
    causal = (later >= earlier)[None, :, :]
    cum_heads = cumulative.T
    dispersion_width = cum_heads[:, :, None] - cum_heads[:, None, :]
    decays = jnp.where(causal, jnp.exp(jnp.where(causal, dispersion_width, 0.0)), 0.0)
    scores = jnp.dot(output_queries, input_keys.T, precision=HIGHEST)
    coupling = decays * scores[None, :, :] * step_sizes.T[:, None, :]
    within = jnp.einsum("hts,shp->thp", coupling, head_values, precision=HIGHEST)
    carried = jnp.exp(cumulative)[:, :, None] * jnp.einsum(
        "tn,hpn->thp", output_queries, entering, precision=HIGHEST
    )
    return within + carried + skip_weights[None, :, None] * head_values


def front_part(hidden, params):
    normed = norm_input(hidden, params[1].astype(jnp.float32)).astype(jnp.bfloat16)
    projected = jnp.dot(normed, params[0], preferred_element_type=jnp.float32)
    return (normed, projected[:, :DI], projected[:, DI:])


def layer_forward(hidden, params, step_sizes, cumulative, totals):
    normed, gate_outputs, mixer_rows = front_part(hidden, params)
    before = passed_along(mixer_rows[-(CONV - 1) :], "seq", 1)
    conv_part = conv_silu(
        before, mixer_rows, params[2].astype(jnp.float32), params[3].astype(jnp.float32)
    )
    head_values, input_keys, output_queries = split_mixer(conv_part)
    summary = block_summary(head_values, input_keys, step_sizes, cumulative)
    entering = carried_in(summary, totals, False)
    mixed = block_output(
        head_values,
        input_keys,
        output_queries,
        step_sizes,
        cumulative,
        entering,
        params[4].astype(jnp.float32),
    )
    mixer_out = mixed.reshape(hidden.shape[0], DI)
    normed_out = gated_norm(mixer_out, gate_outputs, params[5].astype(jnp.float32)).astype(
        jnp.bfloat16
    )
    result = hidden + jnp.dot(normed_out, params[6], preferred_element_type=jnp.float32)
    return (result, before, entering)


def layer_backward(
    hidden, before, entering, step_sizes, cumulative, totals, out_cot, params
):
    length = hidden.shape[0]
    normed, gate_outputs, mixer_rows = front_part(hidden, params)
    kernel = params[2].astype(jnp.float32)
    offset = params[3].astype(jnp.float32)
    conv_part, conv_vjp = jax.vjp(conv_silu, before, mixer_rows, kernel, offset)
    head_values, input_keys, output_queries = split_mixer(conv_part)

    def mixer_fn(values_in, keys_in, queries_in, skip_in):
        mixed_here = block_output(
            values_in, keys_in, queries_in, step_sizes, cumulative, entering, skip_in
        )
        return (mixed_here, block_summary(values_in, keys_in, step_sizes, cumulative))

    (mixed, _), mixer_vjp = jax.vjp(
        mixer_fn, head_values, input_keys, output_queries, params[4].astype(jnp.float32)
    )
    mixer_out = mixed.reshape(length, DI)
    normed_out, norm_vjp = jax.vjp(
        gated_norm, mixer_out, gate_outputs, params[5].astype(jnp.float32)
    )
    out_rounded = normed_out.astype(jnp.bfloat16)
    cot_rounded = out_cot.astype(jnp.bfloat16)
    grad_normed_out = jnp.dot(cot_rounded, params[6].T, preferred_element_type=jnp.float32)
    grad_mixer, grad_gate, grad_gate_gain = norm_vjp(grad_normed_out)
    grad_heads = grad_mixer.reshape(length, HEADS, HEAD_DIM)
    local_entry = jnp.einsum(
        "th,thp,tn->hpn", jnp.exp(cumulative), grad_heads, output_queries, precision=HIGHEST
    )
    leaving = carried_in(local_entry, totals, True)
    grad_values, grad_keys, grad_queries, grad_skip = mixer_vjp((grad_heads, leaving))
    grad_conv = jnp.concatenate([grad_values.reshape(length, DI), grad_keys, grad_queries], axis=1)
    grad_before, grad_rows, grad_kernel, grad_offset = conv_vjp(grad_conv)
    upstream_adjoint = passed_along(grad_before, "seq", -1)
    grad_rows = grad_rows.at[-(CONV - 1) :].add(upstream_adjoint)
    grad_projected = jnp.concatenate([grad_gate, grad_rows], axis=1).astype(jnp.bfloat16)
    grad_normed = jnp.dot(grad_projected, params[0].T, preferred_element_type=jnp.float32)
    _, input_vjp = jax.vjp(norm_input, hidden, params[1].astype(jnp.float32))
    grad_hidden, grad_norm_gain = input_vjp(grad_normed)
    smalls = (grad_norm_gain, grad_kernel, grad_offset, grad_skip, grad_gate_gain)
    factors = (normed, grad_projected, out_rounded, cot_rounded)
    return (out_cot + grad_hidden, smalls, factors)


def packed(parts):
    flat = jnp.concatenate([part.reshape(-1) for part in parts])
    return jnp.pad(flat, (0, -flat.size % 1024))


def swapped(x):
    return lax.ppermute(x, "section", [(0, 1), (1, 0)])


def body(
    inputs,
    out_grad,
    norm_gain,
    input_weight,
    conv_weight,
    conv_bias,
    skip_gain,
    gate_gain,
    out_weight,
    step_codes,
    decay_codes,
):
    section = lax.axis_index("section")
    first = section == 0
    layers = lax.axis_size("section")
    owners = lax.axis_size("fsdp")
    assert layers == 2 and inputs.shape[0] == 2

    def by_layer(mine, theirs):
        return (jnp.where(first, mine, theirs), jnp.where(first, theirs, mine))

    def both_layers(shard):
        rows = shard.shape[0] // layers
        kept = lax.dynamic_slice_in_dim(shard, section * rows, rows, 0)
        sent = lax.dynamic_slice_in_dim(shard, (1 - section) * rows, rows, 0)
        return [
            lax.all_gather(half, ("fsdp", "section"), axis=0, tiled=True)
            for half in by_layer(kept, swapped(sent))
        ]

    in_weights = both_layers(input_weight[0])
    out_weights = both_layers(out_weight[0])
    small_shards = (norm_gain[0], conv_weight[0], conv_bias[0], skip_gain[0], gate_gain[0])
    small_rows = lax.all_gather(packed(small_shards), ("section", "fsdp"))
    small_rows = small_rows.reshape(layers, owners, -1)
    params = []
    for layer in range(layers):
        smalls, at = [], 0
        for shard in small_shards:
            part = small_rows[layer, :, at : at + shard.size].reshape((owners,) + shard.shape)
            at += shard.size
            part = jnp.moveaxis(part, 0, -2)
            smalls.append(part.reshape(part.shape[:-2] + (-1,)))
        params.append((in_weights[layer], *smalls, out_weights[layer]))

    codes = jnp.stack([step_codes[0, :, 0], decay_codes[0, :, 0]], axis=1).astype(jnp.float32)
    here = jnp.where(first, codes[0], codes[1])
    there = jnp.where(first, codes[1], codes[0])
    codes = by_layer(here, swapped(there))
    steps = [code[0] / STEP_SCALE for code in codes]
    cumulatives = [jnp.cumsum(-code[1] / DECAY_SCALE, axis=0) for code in codes]
    totals = lax.all_gather(jnp.stack([part[-1] for part in cumulatives]), "seq")

    hidden = jnp.where(first, inputs[0, 0], inputs[1, 0])
    results, kept_values = [], []
    for layer in range(layers):
        result, before, entering = layer_forward(
            hidden, params[layer], steps[layer], cumulatives[layer], totals[:, layer]
        )
        kept_values.append((hidden, before, entering))
        results.append(result)
        hidden = result

    adjoint = jnp.where(first, out_grad[0, 0], out_grad[1, 0])
    gradients, small_sums, factors, received = [None] * 2, [None] * 2, [None] * 2, [None] * 2
    for layer in reversed(range(layers)):
        adjoint, smalls, factor = layer_backward(
            *kept_values[layer],
            steps[layer],
            cumulatives[layer],
            totals[:, layer],
            adjoint,
            params[layer],
        )
        gradients[layer] = adjoint
        small_sums[layer] = packed(smalls)
        factors[layer] = jnp.concatenate(factor, axis=1)
        received[layer] = lax.ppermute(factors[layer], "section", [(1 - layer, layer)])
    rows = jnp.concatenate(
        [jnp.where(first, factors[0], factors[1]), jnp.where(first, received[0], received[1])],
        axis=0,
    )
    width, projection = params[0][0].shape
    normed_rows = rows[:, :width]
    projected_rows = rows[:, width : width + projection]
    output_rows = rows[:, width + projection : width + projection + DI]
    cotangent_rows = rows[:, width + projection + DI :]
    grad_in = jnp.dot(normed_rows.T, projected_rows, preferred_element_type=jnp.float32)
    grad_out = jnp.dot(output_rows.T, cotangent_rows, preferred_element_type=jnp.float32)
    shares = tuple(
        lax.psum_scatter(
            value.astype(jnp.bfloat16), "fsdp", scatter_dimension=0, tiled=True
        )
        for value in (grad_in, grad_out)
    )
    grad_in, grad_out = lax.psum(shares, "seq")

    summed = lax.psum(jnp.stack(small_sums), ("section", "seq", "fsdp"))
    summed = jnp.where(first, summed[0], summed[1])
    owner, at, small_grads = lax.axis_index("fsdp"), 0, []
    for weight in params[0][1:6]:
        whole = summed[at : at + weight.size].reshape(weight.shape)
        at += weight.size
        share = weight.shape[-1] // owners
        small_grads.append(lax.dynamic_slice_in_dim(whole, owner * share, share, -1))

    def owned(values):
        mine = jnp.where(first, values[0], values[1])
        got = swapped(jnp.where(first, values[1], values[0]))
        return jnp.stack(by_layer(mine, got))

    return (
        owned(results)[None, :, None],
        owned(gradients)[None, :, None],
        small_grads[0][None],
        grad_in.astype(jnp.float32)[None],
        small_grads[1][None],
        small_grads[2][None],
        small_grads[3][None],
        small_grads[4][None],
        grad_out.astype(jnp.float32)[None],
    )


def solution(mesh):
    return jax.shard_map(
        body,
        mesh=mesh,
        in_specs=(
            P(None, "fsdp", "seq", None),
            P(None, "fsdp", "seq", None),
            P("section", "fsdp"),
            P("section", "fsdp", None),
            P("section", None, "fsdp"),
            P("section", "fsdp"),
            P("section", "fsdp"),
            P("section", "fsdp"),
            P("section", "fsdp", None),
            P("section", None, "fsdp", "seq", None),
            P("section", None, "fsdp", "seq", None),
        ),
        out_specs=(
            P("section", None, "fsdp", "seq", None),
            P("section", None, "fsdp", "seq", None),
            P("section", "fsdp"),
            P("section", "fsdp", None),
            P("section", None, "fsdp"),
            P("section", "fsdp"),
            P("section", "fsdp"),
            P("section", "fsdp"),
            P("section", "fsdp", None),
        ),
        check_vma=False,
    )
```

time: 1050 us -> 751 us (0.72)
  blocking collectives: 136 us -> 37.1 us
  local copies, waits for them, and re-layouts: 134 us -> 44.6 us
  matrix products: 158 us -> 86.3 us
  other arithmetic: 80.2 us -> 61.4 us
    psum x1 -> x2, waiting for transfers between devices: 115 us -> 205 us  [the longest x1 129 us: body(): summed = lax.psum(jnp.stack(small_sums), ('section', 'seq', 'fsdp'))]
    all_gather x8, waiting for transfers between devices: 234 us -> 170 us  [the longest x4 96.2 us: both_layers(): lax.all_gather(half, ('fsdp', 'section'), axis=0, tiled=True)]
    all_gather x8 -> x2, blocking collectives: 87.1 us -> 37.1 us  [the longest x1 25 us: body(): small_rows = lax.all_gather(packed(small_shards), ('section', 'fsdp'))]
    slice x1 -> x2, local copies, waits for them, and re-layouts: 37.6 us -> 0.2 us  [conv_silu(): summed = offset[None, :] + kernel[0][None, :] * extended[0:length]]
    reduce_scatter x2, waiting for transfers between devices: 120 us -> 85.2 us  [body(): lax.psum_scatter(value.astype(jnp.bfloat16), 'fsdp', scatter_dimension=0,...]
    unnamed x2 -> x0, blocking collectives: 27.9 us -> none
    select_n x25 -> x10, other arithmetic: 31.8 us -> 7.62 us  [the longest x3 3.29 us: by_layer(): return (jnp.where(first, mine, theirs), jnp.where(first, theirs, mine))]
    psum x1 -> x0, blocking collectives: 20.6 us -> none  [body(): lax.psum((shares[0], shares[1], shares[2], shares[3], shares[4], shares[5...]
  transfers between devices with their start and end apart: 22 -> 23, of which waited for: 17 -> 19; matrix products, arithmetic and copies ran while one was open for 21% -> 16% of each run, Pallas kernels for 0% -> 0%
where the time goes in v1:
time: 751 us; the launch traced here: 741 us
  waiting for transfers between devices  477 us (64%)
  matrix products  86.3 us (11%)
  other arithmetic  61.4 us (8%)
  local copies, waits for them, and re-layouts  44.6 us (6%)
  blocking collectives  37.1 us (5%)
  starting transfers between devices  17.9 us (2%)
  between operations  16.4 us (2%)
    psum x1, waiting for transfers between devices, body(): summed = lax.psum(jnp.stack(small_sums), ('section', 'seq', 'fsdp'))  129 us
    all_gather x4, waiting for transfers between devices, both_layers(): lax.all_gather(half, ('fsdp', 'section'), axis=0, tiled=True)  96.2 us
    reduce_scatter x2, waiting for transfers between devices, body(): lax.psum_scatter(value.astype(jnp.bfloat16), 'fsdp', scatter_dimension=0,...  85.2 us
    psum x1, waiting for transfers between devices, body(): grad_in, grad_out = lax.psum(shares, 'seq')  76.5 us
    all_gather x4, waiting for transfers between devices, carried_in(): pieces = lax.all_gather(local.astype(jnp.bfloat16), 'seq')  73.8 us
    all_gather x1, blocking collectives, body(): small_rows = lax.all_gather(packed(small_shards), ('section', 'fsdp'))  25 us
    dot_general x6, matrix products, block_output(): jnp.einsum('hts,shp->thp', coupling, head_values, precision=HIGHEST)  20.7 us
  transfers between devices with their start and end apart: 23, of which 19 were waited for; matrix products, arithmetic and copies ran while one was open for 16% of the time, Pallas kernels for 0%

profile of v1, /device:TPU:0, one launch (start us, length us, event | category | flops | bytes accessed | tf_op | source)
XLA Modules:
  0.0 740.5 jit_solution(7358947671854968879)
XLA Ops:
  13.0 25.0 %all-gather = bf16[24576]{0:T(1024)(128)(2,1)S(1)} all-gather(bf16[3072]{0:T(1024)(128)(2,1)S(1)} %pad.63), channel_id=2, replica_groups=mesh['section'=2,'seq'=4,'fsdp'=4] {'section','fsdp'}, dimensions={0}, use_global_device_ids=true | all-gather | bytes 55296 | tf_op jit(solution)/shard_map/all_gather | solution.py:216
  41.6 13.7 %all-gather.16.cloned.1.call-done = bf16[768,3328]{1,0:T(8,128)(2,1)} async-done(((bf16[96,3328]{1,0:T(8,128)(2,1)}), bf16[768,3328]{1,0:T(8,128)(2,1)}) %all-gather.16.cloned.1.call-update) | async-done | bytes 5111824 | tf_op jit(solution)/shard_map/all_gather | solution.py:209
  86.4 12.1 %all-gather.6 = f32[4,2,24]{2,1,0:T(2,128)S(1)} all-gather(f32[1,2,24]{2,1,0:T(2,128)S(1)} %maximum_bitcast_fusion.2), channel_id=3, replica_groups=mesh['section'=2,'seq'=4,'fsdp'=4] {'seq'}, dimensions={0}, use_global_device_ids=true | all-gather | bytes 960 | tf_op jit(solution)/shard_map/all_gather | solution.py:234
  101.0 4.1 fusion.10
  105.1 4.0 all-gather.24.cloned.1.call-done
  117.5 21.2 %all-gather.18.cloned.1.call-done = bf16[1536,768]{1,0:T(8,128)(2,1)} async-done(((bf16[192,768]{1,0:T(8,128)(2,1)}), bf16[1536,768]{1,0:T(8,128)(2,1)}) %all-gather.18.cloned.1.call-update) | async-done | bytes 2359312 | tf_op jit(solution)/shard_map/all_gather | solution.py:209
  141.1 40.4 %all-gather.20.cloned.1.call-done = bf16[768,3328]{1,0:T(8,128)(2,1)} async-done(((bf16[96,3328]{1,0:T(8,128)(2,1)}), bf16[768,3328]{1,0:T(8,128)(2,1)}) %all-gather.20.cloned.1.call-update) | async-done | bytes 5111824 | tf_op jit(solution)/shard_map/all_gather | solution.py:209
  186.1 3.7 collective-permute-start.4
  200.8 4.1 fusion.12
  205.0 31.7 %all-gather.26.cloned.1.call-done = bf16[96,64,128]{2,1,0:T(8,128)(2,1)} async-done(((bf16[24,64,128]{2,1,0:T(8,128)(2,1)}), bf16[96,64,128]{2,1,0:T(8,128)(2,1)}) %all-gather.26.cloned.1.call-update) | async-done | bytes 1572880 | tf_op jit(solution)/shard_map/all_gather | solution.py:27
  245.4 20.8 %all-gather.22.cloned.1.call-done = bf16[1536,768]{1,0:T(8,128)(2,1)} async-done(((bf16[192,768]{1,0:T(8,128)(2,1)}), bf16[1536,768]{1,0:T(8,128)(2,1)}) %all-gather.22.cloned.1.call-update) | async-done | bytes 2359312 | tf_op jit(solution)/shard_map/all_gather | solution.py:209
  266.2 3.6 multiply_reduce_fusion.10
  290.0 3.6 fusion.13
  296.2 19.1 %all-gather.28.cloned.1.call-done = bf16[96,64,128]{2,1,0:T(8,128)(2,1)} async-done(((bf16[24,64,128]{2,1,0:T(8,128)(2,1)}), bf16[96,64,128]{2,1,0:T(8,128)(2,1)}) %all-gather.28.cloned.1.call-update) | async-done | bytes 1572880 | tf_op jit(solution)/shard_map/all_gather | solution.py:27
  324.9 4.1 multiply_reduce_fusion.4
  336.5 5.4 multiply_reduce_fusion.18
  369.4 19.0 %all-gather.30.cloned.1.call-done = bf16[96,64,128]{2,1,0:T(8,128)(2,1)} async-done(((bf16[24,64,128]{2,1,0:T(8,128)(2,1)}), bf16[96,64,128]{2,1,0:T(8,128)(2,1)}) %all-gather.30.cloned.1.call-update) | async-done | bytes 1572880 | tf_op jit(solution)/shard_map/all_gather | solution.py:27
  403.2 3.8 collective-permute-done.7
  417.9 3.9 convolution_convert_fusion
  427.3 4.4 multiply_reduce_fusion.19
  433.4 22.0 %reduce-scatter.5.cloned.1.call-done = bf16[384,768]{1,0:T(8,128)(2,1)} async-done(((bf16[1536,768]{1,0:T(8,128)(2,1)}), bf16[384,768]{1,0:T(8,128)(2,1)}) %reduce-scatter.5.cloned.1.call-update) | async-done | bytes 589840 | tf_op jit(solution)/shard_map/reduce_scatter | solution.py:273
  455.4 63.2 %reduce-scatter.3.cloned.1.call-done = bf16[192,3328]{1,0:T(8,128)(2,1)} async-done(((bf16[768,3328]{1,0:T(8,128)(2,1)}), bf16[192,3328]{1,0:T(8,128)(2,1)}) %reduce-scatter.3.cloned.1.call-update) | async-done | bytes 1277968 | tf_op jit(solution)/shard_map/reduce_scatter | solution.py:273
  518.7 128.7 %all-reduce.23.cloned.1.call-done = f32[2,12288]{1,0:T(2,128)} async-done(((f32[2,12288]{1,0:T(2,128)}), f32[2,12288]{1,0:T(2,128)}) %all-reduce.23.cloned.1.call-update) | async-done | bytes 98320 | tf_op jit(solution)/shard_map/psum | solution.py:280
  652.8 76.5 %all-reduce.25.cloned.1.call-done = (bf16[1,192,3328]{2,1,0:T(8,128)(2,1)}, bf16[1,384,768]{2,1,0:T(8,128)(2,1)}) async-done(((bf16[1,192,3328]{2,1,0:T(8,128)(2,1)}, bf16[1,384,768]{2,1,0:T(8,128)(2,1)}), (bf16[1,192,3328]{2,1,0:T(8,128)(2,1)}, bf16[1,384,768]{2,1,0:T(8,128)(2,1)})) %all-reduce.25.cloned.1.call-update) | async-done | bytes 1867792 | tf_op jit(solution)/shard_map/psum | solution.py:278
  (534 shorter events, 185.9 us)
Async XLA Ops:
  7.2 48.1 %all-gather.16.cloned.1.call-start = ((), (), s32[]{:S(2)}) async-start(), calls=%async_computation.2 | async-start | bytes 5750784 | tf_op jit(solution)/shard_map/all_gather | solution.py:209
  8.5 2.3 collective-permute-start
  12.0 97.1 %all-gather.24.cloned.1.call-start = ((), (), s32[]{:S(2)}) async-start(), calls=%async_computation.9 | async-start | bytes 1966080 | tf_op jit(solution)/shard_map/all_gather | solution.py:27
  12.3 28.0 %collective-permute-start.2 = (f32[2,128,24]{2,1,0:T(8,128)S(1)}, f32[2,128,24]{2,1,0:T(8,128)S(1)}, u32[]{:S(2)}, u32[]{:S(2)}) collective-permute-start(f32[2,128,24]{2,1,0:T(8,128)S(1)} %select_bitcast_fusion.4), channel_id=1, source_target_pairs={{0,16},{16,0},{1,17},{17,1},{2,18},{18,2},{3,19},{19,3},{4,20},{20... | collective-permute-start | bytes 73736 | tf_op jit(solution)/shard_map/ppermute | solution.py:179
  38.4 100.4 %copy-start.4 = (f32[1,1,128,768]{3,2,1,0:T(8,128)}, f32[1,1,128,768]{3,2,1,0:T(8,128)S(1)}, u32[]{:S(2)}) copy-start(f32[1,1,128,768]{3,2,1,0:T(8,128)S(1)} %get-tuple-element.124) | copy-start | bytes 1179652
  58.7 4.9 collective-permute-start.1
  70.9 67.8 %all-gather.18.cloned.1.call-start = ((), (), s32[]{:S(2)}) async-start(), calls=%async_computation.3 | async-start | bytes 2654208 | tf_op jit(solution)/shard_map/all_gather | solution.py:209
  72.0 1.8 collective-permute-start.3
  75.8 105.7 %all-gather.20.cloned.1.call-start = ((), (), s32[]{:S(2)}) async-start(), calls=%async_computation.4 | async-start | bytes 5750784 | tf_op jit(solution)/shard_map/all_gather | solution.py:209
  76.4 160.3 %all-gather.26.cloned.1.call-start = ((), (), s32[]{:S(2)}) async-start(), calls=%async_computation.10 | async-start | bytes 1966080 | tf_op jit(solution)/shard_map/all_gather | solution.py:27
  186.1 5.1 collective-permute-start.4
  198.7 67.5 %all-gather.22.cloned.1.call-start = ((), (), s32[]{:S(2)}) async-start(), calls=%async_computation.5 | async-start | bytes 2654208 | tf_op jit(solution)/shard_map/all_gather | solution.py:209
  199.3 116.0 %all-gather.28.cloned.1.call-start = ((), (), s32[]{:S(2)}) async-start(), calls=%async_computation.11 | async-start | bytes 1966080 | tf_op jit(solution)/shard_map/all_gather | solution.py:27
  278.1 110.3 %all-gather.30.cloned.1.call-start = ((), (), s32[]{:S(2)}) async-start(), calls=%async_computation.12 | async-start | bytes 1966080 | tf_op jit(solution)/shard_map/all_gather | solution.py:27
  329.3 5.8 collective-permute-start.6
  352.3 103.1 %reduce-scatter.5.cloned.1.call-start = ((), (), s32[]{:S(2)}) async-start(), calls=%async_computation.8 | async-start | bytes 2949120 | tf_op jit(solution)/shard_map/reduce_scatter | solution.py:273
  357.2 55.6 %collective-permute-start.10 = (bf16[128,6400]{1,0:T(8,128)(2,1)}, bf16[128,6400]{1,0:T(8,128)(2,1)}, u32[]{:S(2)}, u32[]{:S(2)}) collective-permute-start(bf16[128,6400]{1,0:T(8,128)(2,1)} %constant_dynamic-update-slice_fusion.4), channel_id=1, source_target_pairs={{0,16},{1,17},{2,18},{3,19},{4,20},{5,21},{6,22},{7,23},{8,24},{9,... | collective-permute-start | bytes 4915208 | tf_op jit(solution)/shard_map/ppermute | solution.py:260
  401.2 5.8 collective-permute-start.7
  409.8 5.6 collective-permute-start.9
  417.9 100.8 %reduce-scatter.3.cloned.1.call-start = ((), (), s32[]{:S(2)}) async-start(), calls=%async_computation.7 | async-start | bytes 6389760 | tf_op jit(solution)/shard_map/reduce_scatter | solution.py:273
  421.9 225.5 %all-reduce.23.cloned.1.call-start = ((), (), s32[]{:S(2)}) async-start(), calls=%async_computation.6 | async-start | bytes 196608 | tf_op jit(solution)/shard_map/psum | solution.py:280
  422.8 2.9 collective-permute-start.5
  432.6 296.7 %all-reduce.25.cloned.1.call-start = ((), (), s32[]{:S(2)}) async-start(), calls=%async_computation.13 | async-start | bytes 3735552 | tf_op jit(solution)/shard_map/psum | solution.py:278
  432.8 219.0 %collective-permute-start.8 = (f32[128,768]{1,0:T(8,128)S(1)}, f32[128,768]{1,0:T(8,128)S(1)}, u32[]{:S(2)}, u32[]{:S(2)}) collective-permute-start(f32[128,768]{1,0:T(8,128)S(1)} %get-tuple-element.113), channel_id=1, source_target_pairs={{0,16},{16,0},{1,17},{17,1},{2,18},{18,2},{3,19},{19,3},{4,20},{20... | collective-permute-start | bytes 1179656 | tf_op jit(solution)/shard_map/ppermute | solution.py:179
  (149 other events, 1381.9 us)
Sparse Core Ops, SparseCore 0:
  12.1 43.1 all-gather.15
  71.1 37.9 all-gather.23
  111.0 27.7 all-gather.17
  141.0 40.4 all-gather.19
  198.8 37.7 all-gather.25
  238.4 27.7 all-gather.21
  278.2 37.0 all-gather.27
  352.5 35.9 all-gather.29
  418.0 37.4 reduce-scatter.4
  458.4 60.2 reduce-scatter.2
  524.8 122.5 all-reduce.22
  649.7 79.5 all-reduce.24
